TPU v7x, 256 devices: a whole 4x4x8 slice. The times are simulated.
256 devices in a mesh: group: 8 (over x, core), expert: 32 (over z, y).
Axes of the slice: x: 4, y: 4, z: 8, core: 2. Of those that a mesh axis runs over, the one named last changes fastest.
Arguments:
- out_grad: bfloat16 [65536, 3584], P(('group', 'expert')), may hold values from -6 to 6
- gates: float32 [65536, 8], P(('group', 'expert')), may hold values from 0.05 to 0.6
- routes: int32 [65536, 8], P(('group', 'expert')), may hold values from 0 to 95, all different within a row
- copy_pick: int32 [65536, 8], P(('group', 'expert')), may hold values from 0 to 839
- replica_plan: int32 [32], replicated, may hold values from 0 to 23, as said below
- down_weight: bfloat16 [32, 1024, 3584], P('expert'), as said below
- saved_hidden: bfloat16 [8, 32, 32, 20, 1024], P('group', 'expert'), may hold values from -0.75 to 0.75
Outputs:
- route_grad: float32 [65536, 8], P(('group', 'expert'))
- hidden_grad: bfloat16 [8, 32, 32, 20, 1024], P('group', 'expert')
- copy_grad: bfloat16 [32, 1024, 3584], P('expert', 'group')
Inputs may be any that keep to these rules, and one draw needn't show every extreme that they name: `replica_plan`: every expert 0 to 23 is served by at least one slot; exactly 2 experts are served by more than one slot. `down_weight`: slots that serve the same expert hold equal weights.
All inputs are finite; a program needn't handle non-finite values.
Results may differ from a plain program's by a relative error of at most 0.019.
Values may be sent and summed in bfloat16 or wider, within the bound.
A program may use at most 128 MiB of HBM per device.

v0:
```python
import jax
import jax.numpy as jnp
from jax import lax
from jax.sharding import PartitionSpec as P

HOT = 2


def slot_layout(replica_plan):
    slot_count = replica_plan.shape[0]
    slot_ids = jnp.arange(slot_count, dtype=jnp.int32)
    same_expert = replica_plan[:, None] == replica_plan[None, :]
    earlier_slot = slot_ids[None, :] < slot_ids[:, None]
    ordinal = jnp.sum(same_expert & earlier_slot, axis=1)
    return (slot_ids, same_expert, ordinal)


def route_slots(routes, copy_pick, replica_plan, expert_count):
    slot_ids, same_expert, ordinal = slot_layout(replica_plan)
    serves = replica_plan == routes[..., None]
    copies = jnp.sum(serves, axis=-1)
    inside = routes < expert_count
    chosen = copy_pick % jnp.maximum(copies, 1)
    slot_match = serves & (ordinal == chosen[..., None]) & inside[..., None]
    slot_of = jnp.sum(jnp.where(slot_match, slot_ids, 0), axis=-1)
    return (slot_match, slot_of, inside)


def route_ranks(slot_match):
    onehot = slot_match.astype(jnp.int32)
    earlier = jnp.cumsum(onehot, axis=-2) - onehot
    return jnp.sum(earlier * onehot, axis=-1)


def local(out_grad, gates, routes, copy_pick, replica_plan, down_weight, saved_hidden):
    slot_count = replica_plan.shape[0]
    cap_rows = saved_hidden.shape[3]
    expert_count = slot_count - slot_count // 4
    tok_dev, top_count = routes.shape
    model_width = out_grad.shape[1]
    hidden_units = down_weight.shape[1]
    route_count = tok_dev * top_count
    held_count = slot_count * cap_rows
    slot_match, slot_of, inside = route_slots(routes, copy_pick, replica_plan, expert_count)
    route_rank = route_ranks(slot_match.reshape(route_count, slot_count))
    kept_route = inside.reshape(-1) & (route_rank < cap_rows)
    position = jnp.where(kept_route, slot_of.reshape(-1) * cap_rows + route_rank, held_count)
    source_route = (
        jnp.full((held_count,), route_count, jnp.int32)
        .at[position]
        .set(jnp.arange(route_count, dtype=jnp.int32), mode="drop")
    )
    occupied = source_route < route_count
    safe_route = jnp.where(occupied, source_route, 0)
    grad_held = jnp.where(occupied[:, None], out_grad[safe_route // top_count], 0)
    gate_held = jnp.where(occupied, gates.reshape(-1)[safe_route], 0.0).astype(jnp.bfloat16)
    grad_held = grad_held.reshape(slot_count, cap_rows, model_width)
    gate_held = gate_held.reshape(slot_count, cap_rows)
    got_rows, got_gate = (
        lax.all_to_all(grad_held, "expert", split_axis=0, concat_axis=0, tiled=True),
        lax.all_to_all(gate_held, "expert", split_axis=0, concat_axis=0, tiled=True),
    )
    flat_rows = got_rows.reshape(held_count, model_width)
    gate_f = got_gate.reshape(held_count, 1).astype(jnp.float32)
    held_hidden = saved_hidden.reshape(held_count, hidden_units)
    projected = lax.dot_general(
        flat_rows, down_weight[0], (((1,), (1,)), ((), ())), preferred_element_type=jnp.float32
    )
    hidden_grad = (gate_f * projected).astype(jnp.bfloat16)
    route_score = jnp.sum(projected * held_hidden.astype(jnp.float32), axis=1)
    returned = lax.all_to_all(
        route_score.reshape(slot_count, cap_rows), "expert", split_axis=0, concat_axis=0, tiled=True
    )
    score_flat = jnp.concatenate([returned.reshape(-1), jnp.zeros((1,), jnp.float32)])
    route_grad = jnp.where(kept_route, score_flat[position], 0.0).reshape(tok_dev, top_count)
    scaled = (gate_f * flat_rows.astype(jnp.float32)).astype(jnp.bfloat16)
    shard_rows = hidden_units // lax.axis_size("group")
    group_sum = lax.psum_scatter(
        lax.dot_general(
            held_hidden, scaled, (((0,), (0,)), ((), ())), preferred_element_type=jnp.float32
        ).astype(jnp.bfloat16),
        "group",
        scatter_dimension=0,
        tiled=True,
    )
    slot_ids, same_expert, ordinal = slot_layout(replica_plan)
    copies = jnp.sum(same_expert, axis=1)
    hot_first = (copies > 1) & (ordinal == 0)
    hot_rank = jnp.sum(hot_first[None, :] & (replica_plan[None, :] < replica_plan[:, None]), axis=1)
    my_slot = slot_ids == lax.axis_index("expert")
    my_rank = jnp.sum(jnp.where(my_slot, hot_rank, 0))
    my_hot = jnp.any(my_slot & (copies > 1))
    hot_ids = jnp.arange(HOT, dtype=jnp.int32)
    place_hot = (hot_ids == my_rank) & my_hot
    group_f = group_sum.astype(jnp.float32)
    table = jnp.where(place_hot[:, None, None], group_f[None], 0.0)
    summed = lax.psum(table.astype(jnp.bfloat16), "expert").astype(jnp.float32)
    picked = jnp.sum(jnp.where(place_hot[:, None, None], summed, 0.0), axis=0)
    copy_grad = jnp.where(my_hot, picked, group_f).astype(jnp.bfloat16)
    hidden_out = hidden_grad.reshape(1, 1, slot_count, cap_rows, hidden_units)
    return (route_grad, hidden_out, copy_grad.reshape(1, shard_rows, model_width))


def solution(mesh):
    placed = (
        P(("group", "expert"), None),
        P(("group", "expert"), None),
        P(("group", "expert"), None),
        P(("group", "expert"), None),
        P(),
        P("expert", None, None),
        P("group", "expert", None, None, None),
    )
    return jax.shard_map(
        local,
        mesh=mesh,
        in_specs=placed,
        out_specs=(
            P(("group", "expert"), None),
            P("group", "expert", None, None, None),
            P("expert", "group", None),
        ),
        check_vma=False,
    )
```

profile of v0, /device:TPU:2, one launch (start us, length us, event | category | flops | bytes accessed | tf_op | source)
XLA Modules:
  0.0 451.8 jit_solution(13898555410454085809)
XLA Ops:
  7.2 1.0 fusion.9
  8.2 0.8 fusion.4
  9.0 0.8 copy.49
  9.8 0.1 eq.130
  9.9 0.1 eq.115
  10.1 0.1 and.99
  10.3 0.1 and.95
  10.4 0.1 reshape.191
  10.5 0.8 add_select_fusion
  11.3 0.1 copy.51
  11.5 0.1 eq.134
  11.6 0.1 eq.126
  11.7 0.8 copy.60
  12.5 0.1 reshape.195
  12.6 0.9 select_reduce_fusion.1
  13.5 0.1 copy.57
  13.6 0.1 mul.42
  13.8 0.8 and_convert_fusion
  14.6 9.1 %reduce-window.6 = s32[32,16,128]{2,1,0:T(8,128)S(1)} reduce-window(s32[32,16,128]{2,1,0:T(8,128)S(1)} %and_convert_fusion, s32[]{:T(128)} %constant.17.clone.1), window={size=1x1x128 pad=0_0x0_0x127_0}, to_apply=%region_2.3 | reduce-window | flops 8323072 | bytes 524292 | tf_op jit(solution)/shard_map/reduce-window
  23.6 0.1 slice.14
  23.8 0.2 copy.65
  24.0 0.2 reduce-window.9
  24.2 0.1 broadcast_add_fusion
  24.4 0.8 fusion.7
  25.3 8.0 %scatter_custom_fusion = s32[640]{0:T(1024)S(1)} fusion(s32[2048]{0:T(1024)S(1)} %bitcast.45, s32[2048]{0:T(1024)S(1)} %iota.19, s32[]{:T(128)} %constant.20.clone.1), kind=kCustom, calls=%fused_computation.57 | custom fusion | bytes 2564 | tf_op jit(solution)/shard_map/scatter | solution.py:51
  33.3 4.3 gather_fusion.2
  37.7 0.7 all_to_all.20
  38.4 11.5 %all-to-all-start.2 = ((bf16[32,1,20]{2,1,0:T(2,128)(2,1)}), bf16[32,1,20]{2,1,0:T(2,128)(2,1)S(1)}, u32[]{:S(2)}, u32[]{:S(2)}) async-start(bf16[32,1,20]{2,1,0:T(2,128)(2,1)} %all_to_all.20), calls=%async_computation.2 | async-start | bytes 32768 | tf_op jit(solution)/shard_map/all_to_all | solution.py:61
  49.9 0.1 broadcast_in_dim.101
  50.0 5.1 %gather_fusion = bf16[640,3584]{1,0:T(8,128)(2,1)} fusion(bf16[256,3584]{1,0:T(8,128)(2,1)S(1)} %copy-done, s32[1024]{0:T(1024)S(1)} %pad_clamp_fusion.1), kind=kCustom, calls=%fused_computation | custom fusion | bytes 9177600 | tf_op jit(solution)/shard_map/gather | solution.py:55
  55.1 7.3 %gather.14 = bf16[32,20,3584]{2,1,0:T(8,128)(2,1)} reshape(bf16[640,3584]{1,0:T(8,128)(2,1)} %gather_fusion) | data formatting | bytes 9175040 | tf_op jit(solution)/shard_map/gather | solution.py:55
  62.4 5.4 %broadcast_select_fusion = bf16[32,20,3584]{2,1,0:T(8,128)(2,1)} fusion(bf16[32,20,3584]{2,1,0:T(8,128)(2,1)} %gather.14, pred[32,20]{1,0:T(8,128)(4,1)S(1)} %broadcast_in_dim.101), kind=kLoop, calls=%fused_computation.9 | loop fusion | flops 2293760 | bytes 9175680 | tf_op jit(solution)/shard_map/jit(_where)/select_n | solution.py:55
  67.9 9.9 %all-to-all-start = ((bf16[32,20,3584]{2,1,0:T(8,128)(2,1)}), bf16[32,20,3584]{2,1,0:T(8,128)(2,1)}, u32[]{:S(2)}, u32[]{:S(2)}) async-start(bf16[32,20,3584]{2,1,0:T(8,128)(2,1)} %broadcast_select_fusion), calls=%async_computation | async-start | bytes 11010048 | tf_op jit(solution)/shard_map/all_to_all | solution.py:60
  77.8 0.2 reduce-scatter.4.cloned.1.call-start
  78.0 2.1 copy.58
  80.1 1.2 reshape.193
  81.3 118.0 %all-to-all-done = bf16[32,20,3584]{2,1,0:T(8,128)(2,1)} async-done(((bf16[32,20,3584]{2,1,0:T(8,128)(2,1)}), bf16[32,20,3584]{2,1,0:T(8,128)(2,1)}, u32[]{:S(2)}, u32[]{:S(2)}) %all-to-all-start) | async-done | bytes 4587552 | tf_op jit(solution)/shard_map/all_to_all | solution.py:60
  199.3 6.8 %multiply_convert_fusion = bf16[32,20,3584]{2,1,0:T(8,128)(2,1)} fusion(bf16[32,20,3584]{2,1,0:T(8,128)(2,1)} %all-to-all-done, f32[32,20]{1,0:T(8,128)S(1)} %bitcast.41), kind=kLoop, calls=%fused_computation.4 | loop fusion | flops 6881280 | bytes 9177600 | tf_op jit(solution)/shard_map/convert_element_type | solution.py:76
  206.1 7.4 %convert_element_type.91 = bf16[640,3584]{1,0:T(8,128)(2,1)} reshape(bf16[32,20,3584]{2,1,0:T(8,128)(2,1)} %multiply_convert_fusion) | data formatting | bytes 9175040 | tf_op jit(solution)/shard_map/convert_element_type | solution.py:76
  213.4 10.3 %fusion.2 = bf16[1024,3584]{0,1:T(8,128)(2,1)} fusion(bf16[640,3584]{1,0:T(8,128)(2,1)} %convert_element_type.91, bf16[640,1024]{1,0:T(8,128)(2,1)S(1)} %copy-done.3), kind=kOutput, calls=%fused_computation.8 | convolution fusion | flops 4701290496 | bytes 13238272 | tf_op jit(solution)/shard_map/dot_general | solution.py:79
  223.7 10.1 %copy.66 = bf16[1024,3584]{1,0:T(8,128)(2,1)} copy(bf16[1024,3584]{0,1:T(8,128)(2,1)} %fusion.2) | data formatting | bytes 14680064
  233.9 0.6 compare_and_fusion.3
  234.5 0.2 convert_reduce_fusion
  234.7 0.6 fusion.14
  235.3 1.2 compare_and_fusion.2
  236.6 0.1 reshape.198
  236.7 7.3 %reshape.192 = bf16[640,3584]{1,0:T(8,128)(2,1)} reshape(bf16[32,20,3584]{2,1,0:T(8,128)(2,1)} %all-to-all-done) | data formatting | bytes 9175040 | tf_op jit(solution)/shard_map/reshape | solution.py:63
  244.0 38.9 %reduce-scatter.4.cloned.1.call-done = bf16[128,3584]{1,0:T(8,128)(2,1)} async-done(((bf16[1024,3584]{1,0:T(8,128)(2,1)}), bf16[128,3584]{1,0:T(8,128)(2,1)}) %reduce-scatter.4.cloned.1.call-update) | async-done | bytes 917520 | tf_op jit(solution)/shard_map/reduce_scatter | solution.py:78
  282.9 2.7 select_convert_fusion
  285.6 10.5 %multiply_convert_fusion.1 = (bf16[640,1024]{1,0:T(8,128)(2,1)}, f32[640]{0:T(1024)S(1)}) fusion(f32[640]{0:T(1024)S(1)} %reshape.198, bf16[640,1024]{1,0:T(8,128)(2,1)S(1)} %copy-done.3, bf16[640,3584]{1,0:T(8,128)(2,1)} %reshape.192, bf16[1,1024,3584]{2,1,0:T(8,128)(2,1)} %param.12), kind=kOutput, calls=%fused_computation.12 | convolution fusion | flops 4700896768 | bytes 14554112 | tf_op jit(solution)/shard_map/dot_general | solution.py:66
  296.1 0.7 all_to_all.16
  296.9 10.1 %all-to-all-start.1 = ((f32[32,1,20]{2,1,0:T(1,128)}), f32[32,1,20]{2,1,0:T(1,128)S(1)}, u32[]{:S(2)}, u32[]{:S(2)}) async-start(f32[32,1,20]{2,1,0:T(1,128)} %bitcast.6), calls=%async_computation.1 | async-start | bytes 32768 | tf_op jit(solution)/shard_map/all_to_all | solution.py:71
  307.0 0.1 lt.90
  307.1 2.2 reshape.196
  309.3 1.8 copy.64
  311.1 5.7 %all-to-all-done.1 = f32[32,1,20]{2,1,0:T(1,128)S(1)} async-done(((f32[32,1,20]{2,1,0:T(1,128)}), f32[32,1,20]{2,1,0:T(1,128)S(1)}, u32[]{:S(2)}, u32[]{:S(2)}) %all-to-all-start.1) | async-done | bytes 2592 | tf_op jit(solution)/shard_map/all_to_all | solution.py:71
  316.8 0.5 broadcast.191
  317.3 0.7 reduce.7
  318.1 8.6 %gather_fusion.1 = f32[2048]{0:T(1024)S(1)} fusion(f32[641]{0:T(1024)S(1)} %pad_maximum_fusion, s32[2048]{0:T(1024)S(1)} %broadcast_clamp_fusion), kind=kCustom, calls=%fused_computation.1 | custom fusion | bytes 24576 | tf_op jit(solution)/shard_map/gather | solution.py:75
  326.7 0.1 gather.16
  326.9 0.7 copy.63
  327.5 113.8 %all-reduce.2.cloned.1.call-done = bf16[2,128,3584]{2,1,0:T(8,128)(2,1)} async-done(((bf16[2,128,3584]{2,1,0:T(8,128)(2,1)}), bf16[2,128,3584]{2,1,0:T(8,128)(2,1)}) %all-reduce.2.cloned.1.call-update) | async-done | bytes 1835024 | tf_op jit(solution)/shard_map/psum | solution.py:97
  441.3 2.0 select_reduce_fusion
  443.3 1.7 fusion.3
  (32 shorter events, 0.5 us)
Async XLA Ops:
  7.2 42.9 %copy-start = (bf16[256,3584]{1,0:T(8,128)(2,1)S(1)}, bf16[256,3584]{1,0:T(8,128)(2,1)}, u32[]{:S(2)}) copy-start(bf16[256,3584]{1,0:T(8,128)(2,1)} %param.7) | copy-start | bytes 5505028
  38.4 29.5 %all-to-all-start.2 = ((bf16[32,1,20]{2,1,0:T(2,128)(2,1)}), bf16[32,1,20]{2,1,0:T(2,128)(2,1)S(1)}, u32[]{:S(2)}, u32[]{:S(2)}) async-start(bf16[32,1,20]{2,1,0:T(2,128)(2,1)} %all_to_all.20), calls=%async_computation.2 | async-start | bytes 32768 | tf_op jit(solution)/shard_map/all_to_all | solution.py:61
  67.9 131.4 %all-to-all-start = ((bf16[32,20,3584]{2,1,0:T(8,128)(2,1)}), bf16[32,20,3584]{2,1,0:T(8,128)(2,1)}, u32[]{:S(2)}, u32[]{:S(2)}) async-start(bf16[32,20,3584]{2,1,0:T(8,128)(2,1)} %broadcast_select_fusion), calls=%async_computation | async-start | bytes 11010048 | tf_op jit(solution)/shard_map/all_to_all | solution.py:60
  77.8 205.1 %reduce-scatter.4.cloned.1.call-start = ((), (), s32[]{:S(2)}) async-start(), calls=%async_computation.5 | async-start | bytes 8257536 | tf_op jit(solution)/shard_map/reduce_scatter | solution.py:78
  206.1 7.4 %copy-start.3 = (bf16[640,1024]{1,0:T(8,128)(2,1)S(1)}, bf16[640,1024]{1,0:T(8,128)(2,1)}, u32[]{:S(2)}) copy-start(bf16[640,1024]{1,0:T(8,128)(2,1)} %reshape.193) | copy-start | bytes 3932164
  233.8 0.7 copy-start.4
  233.9 207.4 %all-reduce.2.cloned.1.call-start = ((), (), s32[]{:S(2)}) async-start(), calls=%async_computation.4 | async-start | bytes 3670016 | tf_op jit(solution)/shard_map/psum | solution.py:97
  296.9 19.9 %all-to-all-start.1 = ((f32[32,1,20]{2,1,0:T(1,128)}), f32[32,1,20]{2,1,0:T(1,128)S(1)}, u32[]{:S(2)}, u32[]{:S(2)}) async-start(f32[32,1,20]{2,1,0:T(1,128)} %bitcast.6), calls=%async_computation.1 | async-start | bytes 32768 | tf_op jit(solution)/shard_map/all_to_all | solution.py:71
  318.1 125.2 %copy-start.2 = (bf16[128,3584]{1,0:T(8,128)(2,1)S(1)}, bf16[128,3584]{1,0:T(8,128)(2,1)}, u32[]{:S(2)}) copy-start(bf16[128,3584]{1,0:T(8,128)(2,1)} %reduce-scatter.4.cloned.1.call-done) | copy-start | bytes 2752516
  318.1 126.9 %copy-start.1 = (bf16[256,3584]{1,0:T(8,128)(2,1)S(1)}, bf16[256,3584]{1,0:T(8,128)(2,1)}, u32[]{:S(2)}) copy-start(bf16[256,3584]{1,0:T(8,128)(2,1)} %param.7) | copy-start | bytes 5505028
Sparse Core Ops, SparseCore 0:
  234.0 48.8 reduce-scatter.3
  286.4 154.8 all-reduce.1
where the time goes:
time: 453 us; the launch traced here: 452 us
  waiting for transfers between devices  276 us (61%)
  local copies, waits for them, and re-layouts  71.8 us (16%)
  other arithmetic  36.7 us (8%)
  starting transfers between devices  31.7 us (7%)
  matrix products  20.8 us (5%)
  between operations  14.4 us (3%)
    all_to_all x1, waiting for transfers between devices, local(): lax.all_to_all(grad_held, 'expert', split_axis=0, concat_axis=0, tiled=True)  118 us
    psum x1, waiting for transfers between devices, local(): summed = lax.psum(table.astype(jnp.bfloat16), 'expert').astype(jnp.float32)  114 us
    reduce_scatter x1, waiting for transfers between devices, local(): lax.psum_scatter(lax.dot_general(held_hidden, scaled, (((0,), (0,)), ((),...  38.9 us
    unnamed x16, local copies, waits for them, and re-layouts  16.3 us
    gather x2, local copies, waits for them, and re-layouts, local(): out_grad[safe_route // top_count]  12.4 us
    all_to_all x1, starting transfers between devices, local(): lax.all_to_all(gate_held, 'expert', split_axis=0, concat_axis=0, tiled=True)  11.5 us
    dot_general x1, matrix products, local(): lax.dot_general(flat_rows, down_weight[0], (((1,), (1,)), ((), ())), pref...  10.5 us
    dot_general x1, matrix products, local(): lax.dot_general(held_hidden, scaled, (((0,), (0,)), ((), ())), preferred_...  10.3 us
  transfers between devices with their start and end apart: 5, of which 4 were waited for; matrix products, arithmetic and copies ran while one was open for 13% of the time, Pallas kernels for 0%

commit v1 on v0

v1 whole, which is shorter than its diff:
```python
import functools

import jax
import jax.numpy as jnp
from jax import lax
from jax.experimental import pallas as pl
from jax.experimental.pallas import tpu as pltpu
from jax.sharding import PartitionSpec as P

CORES = 2
YS = 4
LANES = 128
HEAD = 16
CHUNK = 512
COLS = CHUNK + LANES
MESH = pl.DeviceIdType.MESH
F32 = jnp.float32
BF16 = jnp.bfloat16


def iota(shape, dim):
    return lax.broadcasted_iota(jnp.int32, shape, dim)


def mm(a, b):
    return lax.dot_general(a, b, (((1,), (0,)), ((), ())), preferred_element_type=F32)


def mm_nt(a, b):
    return lax.dot_general(a, b, (((1,), (1,)), ((), ())), preferred_element_type=F32)


def onehot(mask):
    return jnp.where(mask, 1.0, 0.0).astype(BF16)


def kernel(
    dims,
    og_hbm,
    w_hbm,
    h_hbm,
    gates_ref,
    routes_ref,
    pick_ref,
    plan_ref,
    rg_ref,
    hg_ref,
    cg_ref,
    og_v,
    w_v,
    h_v,
    hq,
    ht,
    s_head,
    s_tail,
    shuffle,
    sbuf,
    rbuf,
    gate_out,
    gate_in,
    score_out,
    score_in,
    rows_b,
    scaled_b,
    gcol,
    proj,
    hg_v,
    pb,
    pr,
    xb,
    xr,
    gsum,
    yr,
    tb,
    zr,
    ub,
    vb,
    wb,
    ya,
    ld_sem,
    own_sem,
    row_s,
    row_r,
    gate_s,
    gate_r,
    pair_s,
    pair_r,
    x_s,
    x_r,
    y_s,
    y_r,
    z_s,
    z_r,
    v_s,
    v_r,
    w_s,
    w_r,
    score_s,
    score_r,
):
    groups, slots, cap, toks, topk, width, hidden = dims
    xs, zs = groups // CORES, slots // YS
    tail = cap - HEAD
    chunks = width // CHUNK
    n_head, n_tail = slots * HEAD, slots * tail
    n_rows = n_head + n_tail
    piece = hidden // groups
    zrows = piece // zs
    ycols = CHUNK // YS

    g = lax.axis_index("group")
    e = lax.axis_index("expert")
    x, core = g // CORES, g % CORES
    z, y = e // YS, e % YS
    mate = (x * CORES + (1 - core), e)

    def plane(k):
        return (g, lax.rem(z + k // YS, zs) * YS + lax.rem(y + k % YS, YS))

    def plane_slot(k):
        return lax.rem(z + k // YS, zs) * YS + lax.rem(y + k % YS, YS)

    def xdev(k):
        return (lax.rem(x + k, xs) * CORES + core, e)

    def ydev(k):
        return (g, z * YS + lax.rem(y + k, YS))

    def zdev(k):
        return (g, lax.rem(z + k, zs) * YS + y)

    def remote(src, dst, ssem, rsem, dev):
        pltpu.make_async_remote_copy(
            src_ref=src, dst_ref=dst, send_sem=ssem, recv_sem=rsem, device_id=dev, device_id_type=MESH
        ).start()

    def await_bytes(ref, sem):
        pltpu.make_async_copy(ref, ref, sem).wait()

    ld_og = pltpu.make_async_copy(og_hbm, og_v, ld_sem.at[0])
    ld_h = pltpu.make_async_copy(h_hbm, h_v, ld_sem.at[1])
    ld_w = pltpu.make_async_copy(w_hbm, w_v, ld_sem.at[2])
    ld_og.start()
    ld_h.start()
    ld_w.start()

    barrier = pltpu.get_barrier_semaphore()

    def greet(k, carry):
        pl.semaphore_signal(barrier, inc=1, device_id=plane(k), device_id_type=MESH)
        return carry

    lax.fori_loop(1, slots, greet, 0)
    pl.semaphore_signal(barrier, inc=1, device_id=mate, device_id_type=MESH)
    for k in range(1, xs):
        pl.semaphore_signal(barrier, inc=1, device_id=xdev(k), device_id_type=MESH)

    plan_row = plan_ref[...].astype(F32)
    si, ti = iota((slots, slots), 0), iota((slots, slots), 1)
    plan_col = jnp.sum(jnp.where(si == ti, plan_row, 0.0), axis=1, keepdims=True)
    same = jnp.where(plan_col == plan_row, 1.0, 0.0)
    reps_col = jnp.sum(same, axis=1, keepdims=True)
    reps_row = jnp.sum(same, axis=0, keepdims=True)
    ord_col = jnp.sum(jnp.where(ti < si, same, 0.0), axis=1, keepdims=True)
    ord_row = jnp.sum(jnp.where(si < ti, same, 0.0), axis=0, keepdims=True)
    first_row = jnp.where((reps_row > 1.0) & (ord_row == 0.0), 1.0, 0.0)
    hot_rank = jnp.sum(jnp.where(plan_row < plan_col, first_row, 0.0), axis=1, keepdims=True)
    slot_id = iota((slots, 1), 0)

    def at_slot(col, slot):
        return jnp.sum(jnp.where(slot_id == slot, col, 0.0), axis=0, keepdims=True)

    in_table = [jnp.where((reps_col > 1.0) & (hot_rank == float(h)), 1.0, 0.0) for h in range(2)]
    y_weight = [[at_slot(in_table[h], z * YS + yy) for h in range(2)] for yy in range(YS)]
    my_hot = at_slot(in_table[0] + in_table[1], e) > 0.0

    inv_reps = 1.0 / reps_col

    def match(k):
        route = routes_ref[k : k + 1, :].astype(F32)
        pick = pick_ref[k : k + 1, :].astype(F32)
        chosen = pick - jnp.floor((pick + 0.5) * inv_reps) * reps_col
        return (plan_col == route) & (chosen == ord_col)

    taken = jnp.zeros((slots, toks), F32)
    gate_of = jnp.zeros((slots, toks), F32)
    for k in range(topk):
        hit = match(k)
        taken = jnp.where(hit, 1.0, taken)
        gate_of = jnp.where(hit, gates_ref[k : k + 1, :], gate_of)
    before = onehot(iota((toks, toks), 0) < iota((toks, toks), 1))
    rank = mm(taken.astype(BF16), before)
    rank = jnp.where((taken > 0.0) & (rank < float(cap)), rank, 64.0)
    rank_b, gate_b = rank.astype(BF16), gate_of.astype(BF16)
    grow = jnp.zeros((slots, LANES), F32)
    for per, base, s_ref in ((HEAD, 0, s_head), (tail, HEAD, s_tail)):
        n = slots * per
        spread = onehot(iota((n, slots), 0) // per == iota((n, slots), 1))
        collect = onehot(iota((slots, n), 1) // per == iota((slots, n), 0))
        c_of = iota((n, 1), 0) % per + base
        sel = jnp.where(mm(spread, rank_b) == c_of.astype(F32), 1.0, 0.0)
        s_ref[...] = sel.astype(BF16)
        held = jnp.sum(sel * mm(spread, gate_b), axis=1, keepdims=True)
        grow = grow + mm(collect, jnp.where(iota((n, LANES), 1) == c_of, held, 0.0).astype(BF16))
    for s in range(slots):
        gate_out[s] = grow[s : s + 1, :]

    blocks = CHUNK // LANES
    rr, cc = iota((n_head, n_head), 0), iota((n_head, n_head), 1)
    shuffle[...] = onehot(cc == (rr // tail % blocks) * n_tail + (rr // HEAD) * tail + rr % tail)

    ld_og.wait()

    def gather(c):
        part = og_v[:, pl.ds(pl.multiple_of(c * CHUNK, CHUNK), CHUNK)]
        sbuf[c, :, :, 0:CHUNK] = mm(s_head[...], part).astype(BF16).reshape(slots, HEAD, CHUNK)
        low = mm(s_tail[...], part).astype(BF16)
        low = jnp.concatenate([low[:, i * LANES : (i + 1) * LANES] for i in range(blocks)], axis=0)
        sbuf[c, :, :, CHUNK:COLS] = mm(shuffle[...], low).astype(BF16).reshape(slots, HEAD, LANES)

    gather(0)
    pl.semaphore_wait(barrier, slots + xs - 1)

    def send_gate(k, carry):
        remote(gate_out.at[plane_slot(k)], gate_in.at[e], gate_s, gate_r, plane(k))
        return carry

    def dispatch(c, carry):
        def one(k, inner):
            remote(sbuf.at[c, plane_slot(k)], rbuf.at[c, e], row_s.at[c], row_r.at[c], plane(k))
            return inner

        lax.fori_loop(1, slots, one, 0)
        pltpu.make_async_copy(sbuf.at[c, e], rbuf.at[c, e], own_sem.at[c]).start()

        @pl.when(c + 1 < chunks)
        def _():
            gather(c + 1)

        return carry

    lax.fori_loop(1, slots, send_gate, 0)
    own_gate = pltpu.make_async_copy(gate_out.at[e], gate_in.at[e], ld_sem.at[3])
    own_gate.start()
    lax.fori_loop(0, chunks, dispatch, 0)

    ld_h.wait()
    fb = min(256, hidden)

    def order(per, back):
        n = slots * per
        r, c = iota((n, n), 0), iota((n, n), 1)
        if back:
            return onehot(c == (r % slots) * per + r // slots)
        return onehot(c == (r % per) * slots + r // per)

    fwd_head, fwd_tail = order(HEAD, False), order(tail, False)

    def reorder(f, carry):
        cols = pl.ds(pl.multiple_of(f * fb, fb), fb)
        hq[0:n_head, cols] = mm(fwd_head, h_v[0:n_head, cols]).astype(BF16)
        hq[n_head:n_rows, cols] = mm(fwd_tail, h_v[n_head:n_rows, cols]).astype(BF16)
        ht[cols, :] = hq[:, cols].T
        return carry

    lax.fori_loop(0, hidden // fb, reorder, 0)
    proj[...] = jnp.zeros_like(proj)

    await_bytes(gate_in.at[pl.ds(0, slots - 1)], gate_r)
    own_gate.wait()
    gin = gate_in[:, 0, :].astype(BF16)
    for per, base, first in ((HEAD, 0, 0), (tail, HEAD, n_head)):
        n = slots * per
        spread = onehot(iota((n, slots), 0) // per == iota((n, slots), 1))
        c_of = iota((n, 1), 0) % per + base
        picked = jnp.where(iota((n, LANES), 1) == c_of, mm(spread, gin), 0.0)
        gcol[first : first + n, :] = jnp.sum(picked, axis=1, keepdims=True)
    ld_w.wait()
    xb_rows = CORES * piece

    def from_x(c):
        await_bytes(xr.at[c], x_r.at[c])
        total = xb[c, x].astype(F32)
        for k in range(xs - 1):
            total = total + xr[c, k].astype(F32)
        total = total.astype(BF16)
        for yy in range(YS):
            gsum[c, yy] = total[:, yy * ycols : (yy + 1) * ycols]
        for k in range(1, YS):
            remote(gsum.at[c, lax.rem(y + k, YS)], yr.at[c, k - 1], y_s.at[c], y_r.at[c], ydev(k))

    def from_y(c):
        await_bytes(yr.at[c], y_r.at[c])
        for h in range(2):
            total = jnp.zeros((piece, ycols), F32)
            for yy in range(YS):
                came = gsum[c, y].astype(F32)
                for k in range(1, YS):
                    came = jnp.where(lax.rem(y + YS - k, YS) == yy, yr[c, k - 1].astype(F32), came)
                total = total + y_weight[yy][h] * came
            tb[c, :, h] = total.astype(BF16).reshape(zs, zrows, ycols)
        for k in range(1, zs):
            remote(tb.at[c, lax.rem(z + k, zs)], zr.at[c, k - 1], z_s.at[c], z_r.at[c], zdev(k))

    def from_z(c):
        await_bytes(zr.at[c], z_r.at[c])
        total = tb[c, z].astype(F32)
        for k in range(zs - 1):
            total = total + zr[c, k].astype(F32)
        total = total.astype(BF16)
        ub[c] = total
        vb[c, z] = total
        for k in range(1, zs):
            remote(ub.at[c], vb.at[c, z], v_s.at[c], v_r.at[c], zdev(k))

    def from_v(c):
        await_bytes(vb.at[c, pl.ds(0, zs - 1)], v_r.at[c])
        tables = [vb[c, :, h].reshape(piece, ycols).astype(F32) for h in range(2)]
        for yy in range(YS):
            wb[c, yy] = (y_weight[yy][0] * tables[0] + y_weight[yy][1] * tables[1]).astype(BF16)
        ya[c, y] = wb[c, y]
        for k in range(1, YS):
            remote(wb.at[c, lax.rem(y + k, YS)], ya.at[c, y], w_s.at[c], w_r.at[c], ydev(k))

    def from_w(c):
        await_bytes(ya.at[c, pl.ds(0, YS - 1)], w_r.at[c])
        for yy in range(YS):
            cols = pl.ds(pl.multiple_of(c * CHUNK + yy * ycols, ycols), ycols)
            cg_ref[:, cols] = jnp.where(my_hot, ya[c, yy].astype(F32), gsum[c, yy].astype(F32)).astype(BF16)

    def main(c, carry):
        await_bytes(rbuf.at[c, pl.ds(0, slots - 1)], row_r.at[c])
        pltpu.make_async_copy(sbuf.at[c, e], rbuf.at[c, e], own_sem.at[c]).wait()
        rows_b[0:n_head, :] = rbuf[c, :, :, 0:CHUNK].reshape(n_head, CHUNK)
        low = lax.dot_general(
            shuffle[...],
            rbuf[c, :, :, CHUNK:COLS].reshape(n_head, LANES),
            (((0,), (0,)), ((), ())),
            preferred_element_type=F32,
        ).astype(BF16)
        for i in range(blocks):
            rows_b[n_head:n_rows, i * LANES : (i + 1) * LANES] = low[i * n_tail : (i + 1) * n_tail, :]
        scaled_b[...] = (gcol[...] * rows_b[...].astype(F32)).astype(BF16)

        def partial(xx, inner):
            rows = pl.ds(pl.multiple_of(xx * xb_rows, xb_rows), xb_rows)
            out = mm(ht[rows, :], scaled_b[...]).astype(BF16)
            for cc in range(CORES):
                pb[c, cc, xx] = out[cc * piece : (cc + 1) * piece, :]
            return inner

        lax.fori_loop(0, xs, partial, 0)
        remote(pb.at[c, 1 - core], pr.at[c], pair_s.at[c], pair_r.at[c], mate)

        def accumulate(f, inner):
            rows = pl.ds(pl.multiple_of(f * fb, fb), fb)
            wcols = pl.ds(pl.multiple_of(c * CHUNK, CHUNK), CHUNK)
            proj[:, rows] += mm_nt(rows_b[...], w_v[rows, wcols])
            return inner

        lax.fori_loop(0, hidden // fb, accumulate, 0)

        await_bytes(pr.at[c], pair_r.at[c])
        for xx in range(xs):
            xb[c, xx] = (pb[c, core, xx].astype(F32) + pr[c, xx].astype(F32)).astype(BF16)
        for k in range(1, xs):
            remote(xb.at[c, lax.rem(x + k, xs)], xr.at[c, k - 1], x_s.at[c], x_r.at[c], xdev(k))

        @pl.when(c >= 1)
        def _():
            from_x(c - 1)

        return carry

    lax.fori_loop(0, chunks, main, 0)

    back_head, back_tail = order(HEAD, True), order(tail, True)

    def finish(f, score):
        cols = pl.ds(pl.multiple_of(f * fb, fb), fb)
        block = proj[:, cols]
        grad = (gcol[...] * block).astype(BF16)
        hg_v[0:n_head, cols] = mm(back_head, grad[0:n_head, :]).astype(BF16)
        hg_v[n_head:n_rows, cols] = mm(back_tail, grad[n_head:n_rows, :]).astype(BF16)
        return score + jnp.sum(block * hq[:, cols].astype(F32), axis=1, keepdims=True)

    score = lax.fori_loop(0, hidden // fb, finish, jnp.zeros((n_rows, 1), F32))
    srow = jnp.zeros((slots, LANES), F32)
    for per, base, first in ((HEAD, 0, 0), (tail, HEAD, n_head)):
        n = slots * per
        collect = jnp.where(iota((slots, n), 1) // per == iota((slots, n), 0), 1.0, 0.0)
        c_of = iota((n, 1), 0) % per + base
        put = jnp.where(iota((n, LANES), 1) == c_of, score[first : first + n, :], 0.0)
        srow = srow + lax.dot_general(
            collect, put, (((1,), (0,)), ((), ())), precision=lax.Precision.HIGHEST, preferred_element_type=F32
        )
    for s in range(slots):
        score_out[s] = srow[s : s + 1, :]

    def send_score(k, carry):
        remote(score_out.at[plane_slot(k)], score_in.at[e], score_s, score_r, plane(k))
        return carry

    lax.fori_loop(1, slots, send_score, 0)
    own_score = pltpu.make_async_copy(score_out.at[e], score_in.at[e], ld_sem.at[4])
    own_score.start()
    out_h = pltpu.make_async_copy(hg_v, hg_ref, ld_sem.at[5])
    out_h.start()

    from_x(chunks - 1)

    def each(stage):
        def run(c, carry):
            stage(c)
            return carry

        lax.fori_loop(0, chunks, run, 0)

    each(from_y)
    each(from_z)
    each(from_v)
    each(from_w)

    await_bytes(score_in.at[pl.ds(0, slots - 1)], score_r)
    own_score.wait()
    sin = score_in[:, 0, :]
    value = jnp.zeros((slots, toks), F32)
    for c in range(cap):
        value = jnp.where(rank == float(c), sin[:, c : c + 1], value)
    for k in range(topk):
        rg_ref[k : k + 1, :] = jnp.sum(jnp.where(match(k), value, 0.0), axis=0, keepdims=True)

    out_h.wait()
    await_bytes(gate_out.at[pl.ds(0, slots - 1)], gate_s)
    await_bytes(score_out.at[pl.ds(0, slots - 1)], score_s)

    def settle(c, carry):
        await_bytes(sbuf.at[c, pl.ds(0, slots - 1)], row_s.at[c])
        await_bytes(pr.at[c], pair_s.at[c])
        await_bytes(xr.at[c], x_s.at[c])
        await_bytes(yr.at[c], y_s.at[c])
        await_bytes(zr.at[c], z_s.at[c])
        await_bytes(zr.at[c], v_s.at[c])
        await_bytes(yr.at[c], w_s.at[c])
        return carry

    lax.fori_loop(0, chunks, settle, 0)


def local(groups, slots, out_grad, gates, routes, copy_pick, replica_plan, down_weight, saved_hidden):
    toks, width = out_grad.shape
    topk = routes.shape[1]
    hidden = down_weight.shape[1]
    cap = saved_hidden.shape[3]
    xs, zs = groups // CORES, slots // YS
    tail = cap - HEAD
    chunks = width // CHUNK
    n_rows = slots * cap
    n_head = slots * HEAD
    piece = hidden // groups
    zrows = piece // zs
    ycols = CHUNK // YS
    held = saved_hidden[0, 0].transpose(1, 0, 2).reshape(n_rows, hidden)
    vmem = pltpu.VMEM
    dma = pltpu.SemaphoreType.DMA
    scratch = [
        vmem((toks, width), BF16),
        vmem((hidden, width), BF16),
        vmem((n_rows, hidden), BF16),
        vmem((n_rows, hidden), BF16),
        vmem((hidden, n_rows), BF16),
        vmem((n_head, toks), BF16),
        vmem((slots * tail, toks), BF16),
        vmem((n_head, n_head), BF16),
        vmem((chunks, slots, HEAD, COLS), BF16),
        vmem((chunks, slots, HEAD, COLS), BF16),
        vmem((slots, 1, LANES), F32),
        vmem((slots, 1, LANES), F32),
        vmem((slots, 1, LANES), F32),
        vmem((slots, 1, LANES), F32),
        vmem((n_rows, CHUNK), BF16),
        vmem((n_rows, CHUNK), BF16),
        vmem((n_rows, 1), F32),
        vmem((n_rows, hidden), F32),
        vmem((n_rows, hidden), BF16),
        vmem((chunks, CORES, xs, piece, CHUNK), BF16),
        vmem((chunks, xs, piece, CHUNK), BF16),
        vmem((chunks, xs, piece, CHUNK), BF16),
        vmem((chunks, xs - 1, piece, CHUNK), BF16),
        vmem((chunks, YS, piece, ycols), BF16),
        vmem((chunks, YS - 1, piece, ycols), BF16),
        vmem((chunks, zs, 2, zrows, ycols), BF16),
        vmem((chunks, zs - 1, 2, zrows, ycols), BF16),
        vmem((chunks, 2, zrows, ycols), BF16),
        vmem((chunks, zs, 2, zrows, ycols), BF16),
        vmem((chunks, YS, piece, ycols), BF16),
        vmem((chunks, YS, piece, ycols), BF16),
        dma((6,)),
        dma((chunks,)),
        dma((chunks,)),
        dma((chunks,)),
        dma,
        dma,
        dma((chunks,)),
        dma((chunks,)),
        dma((chunks,)),
        dma((chunks,)),
        dma((chunks,)),
        dma((chunks,)),
        dma((chunks,)),
        dma((chunks,)),
        dma((chunks,)),
        dma((chunks,)),
        dma((chunks,)),
        dma((chunks,)),
        dma,
        dma,
    ]
    dims = (groups, slots, cap, toks, topk, width, hidden)
    here = pl.BlockSpec(memory_space=pltpu.VMEM)
    there = pl.BlockSpec(memory_space=pl.ANY)
    route_grad, hidden_grad, copy_grad = pl.pallas_call(
        functools.partial(kernel, dims),
        out_shape=(
            jax.ShapeDtypeStruct((topk, toks), F32),
            jax.ShapeDtypeStruct((n_rows, hidden), BF16),
            jax.ShapeDtypeStruct((piece, width), BF16),
        ),
        in_specs=[there, there, there, here, here, here, here],
        out_specs=(here, there, here),
        scratch_shapes=scratch,
        compiler_params=pltpu.CompilerParams(
            collective_id=0, has_side_effects=True, vmem_limit_bytes=63 * 2**20
        ),
        name="expert_backward",
    )(out_grad, down_weight[0], held, gates.T, routes.T, copy_pick.T, replica_plan[None, :])
    hidden_grad = hidden_grad.reshape(cap, slots, hidden).transpose(1, 0, 2)
    return route_grad.T, hidden_grad[None, None], copy_grad[None]


def solution(mesh):
    groups, slots = mesh.shape["group"], mesh.shape["expert"]
    placed = (
        P(("group", "expert"), None),
        P(("group", "expert"), None),
        P(("group", "expert"), None),
        P(("group", "expert"), None),
        P(),
        P("expert", None, None),
        P("group", "expert", None, None, None),
    )
    return jax.shard_map(
        functools.partial(local, groups, slots),
        mesh=mesh,
        in_specs=placed,
        out_specs=(
            P(("group", "expert"), None),
            P("group", "expert", None, None, None),
            P("expert", "group", None),
        ),
        check_vma=False,
    )
```

time: 453 us -> 164 us (0.36)
  waiting for transfers between devices: 276 us -> 0 us
  Pallas kernels: 0 us -> 156 us
  local copies, waits for them, and re-layouts: 71.8 us -> 4.81 us
  other arithmetic: 36.7 us -> 0 us
  starting transfers between devices: 31.7 us -> 0 us
  matrix products: 20.8 us -> 0 us
  between operations: 14.4 us -> 0.64 us
    pallas_call x0 -> x1, Pallas kernels: none -> 156 us  [local(): pl.pallas_call(functools.partial(kernel, dims), out_shape=(jax.ShapeDtype...]
    all_to_all x3 -> x0, waiting for transfers between devices: 124 us -> none  [the longest x1 118 us: local(): lax.all_to_all(grad_held, 'expert', split_axis=0, concat_axis=0, tiled=True)]
    psum x1 -> x0, waiting for transfers between devices: 114 us -> none  [local(): summed = lax.psum(table.astype(jnp.bfloat16), 'expert').astype(jnp.float32)]
    reduce_scatter x1 -> x0, waiting for transfers between devices: 38.9 us -> none  [local(): lax.psum_scatter(lax.dot_general(held_hidden, scaled, (((0,), (0,)), ((),...]
    all_to_all x3 -> x0, starting transfers between devices: 31.5 us -> none  [the longest x1 11.5 us: local(): lax.all_to_all(gate_held, 'expert', split_axis=0, concat_axis=0, tiled=True)]
    gather x5 -> x0, local copies, waits for them, and re-layouts: 25.4 us -> none  [the longest x2 12.4 us: local(): out_grad[safe_route // top_count]]
    dot_general x2 -> x0, matrix products: 20.8 us -> none  [the longest x1 10.5 us: local(): lax.dot_general(flat_rows, down_weight[0], (((1,), (1,)), ((), ())), pref...]
    unnamed x16 -> x5, local copies, waits for them, and re-layouts: 16.3 us -> 4.81 us
  transfers between devices with their start and end apart: 5 -> 0, of which waited for: 4 -> 0; matrix products, arithmetic and copies ran while one was open for 13% -> 0% of each run, Pallas kernels for 0% -> 0%
where the time goes in v1:
time: 164 us; the launch traced here: 162 us
  Pallas kernels  156 us (95%)
  local copies, waits for them, and re-layouts  4.81 us (3%)
    pallas_call x1, Pallas kernels, local(): pl.pallas_call(functools.partial(kernel, dims), out_shape=(jax.ShapeDtype...  156 us
    unnamed x5, local copies, waits for them, and re-layouts  4.81 us

profile of v1, /device:TPU:2, one launch (start us, length us, event | category | flops | bytes accessed | tf_op | source)
XLA Modules:
  0.0 161.6 jit_solution(868888219729074961)
XLA Ops:
  0.6 156.2 %expert_backward.1 = (f32[8,256]{1,0:T(8,128)}, bf16[640,1024]{1,0:T(8,128)(2,1)}, bf16[128,3584]{1,0:T(8,128)(2,1)}) custom-call(bf16[256,3584]{1,0:T(8,128)(2,1)} %og_hbm.1, bf16[1024,3584]{1,0:T(8,128)(2,1)} %bitcast.17, bf16[640,1024]{1,0:T(8,128)(2,1)} %bitcast.18, f32[8,256]{1,0:T(8,128)} %bitcast.21, s32[8,256]{1,0:T(8,128)} %bitcast.22, ...), custom_call_target="tpu_custom_call" | custom-call | tf_op jit(solution)/shard_map/expert_backward/pallas_call | solution.py:522
  156.8 1.3 copy.13
  158.1 0.0 copy-start
  158.1 2.6 %copy.14 = bf16[1,1,32,20,1024]{4,2,3,1,0:T(8,128)(2,1)} copy(bf16[1,1,32,20,1024]{4,2,3,1,0:T(8,128)(2,1)} %bitcast.19) | data formatting | bytes 2621440
  160.7 0.0 copy-done
  160.7 0.9 copy.15
Async XLA Ops:
  158.1 2.6 %copy-start = (bf16[128,3584]{1,0:T(8,128)(2,1)S(1)}, bf16[128,3584]{1,0:T(8,128)(2,1)}, u32[]{:S(2)}) copy-start(bf16[128,3584]{1,0:T(8,128)(2,1)} %get-tuple-element.8) | copy-start | bytes 2752516

commit v2 on v1

--- a/solution.py
+++ b/solution.py
@@ -172,6 +172,7 @@
 
     in_table = [jnp.where((reps_col > 1.0) & (hot_rank == float(h)), 1.0, 0.0) for h in range(2)]
     y_weight = [[at_slot(in_table[h], z * YS + yy) for h in range(2)] for yy in range(YS)]
+    near_weight = [[at_slot(in_table[h], z * YS + lax.rem(y + YS - k, YS)) for h in range(2)] for k in range(YS)]
     my_hot = at_slot(in_table[0] + in_table[1], e) > 0.0
 
     inv_reps = 1.0 / reps_col
@@ -192,22 +193,23 @@
     rank = mm(taken.astype(BF16), before)
     rank = jnp.where((taken > 0.0) & (rank < float(cap)), rank, 64.0)
     rank_b, gate_b = rank.astype(BF16), gate_of.astype(BF16)
-    grow = jnp.zeros((slots, LANES), F32)
-    for per, base, s_ref in ((HEAD, 0, s_head), (tail, HEAD, s_tail)):
+    parts = ((HEAD, 0, 0, s_head), (tail, HEAD, n_head, s_tail))
+
+    def spread(per):
         n = slots * per
-        spread = onehot(iota((n, slots), 0) // per == iota((n, slots), 1))
-        collect = onehot(iota((slots, n), 1) // per == iota((slots, n), 0))
-        c_of = iota((n, 1), 0) % per + base
-        sel = jnp.where(mm(spread, rank_b) == c_of.astype(F32), 1.0, 0.0)
-        s_ref[...] = sel.astype(BF16)
-        held = jnp.sum(sel * mm(spread, gate_b), axis=1, keepdims=True)
-        grow = grow + mm(collect, jnp.where(iota((n, LANES), 1) == c_of, held, 0.0).astype(BF16))
-    for s in range(slots):
-        gate_out[s] = grow[s : s + 1, :]
+        return onehot(iota((n, 1), 0) // per == iota((n, slots), 1))
+
+    def rank_of(per, base):
+        return iota((slots * per, 1), 0) % per + base
+
+    for per, base, _, s_ref in parts:
+        s_ref[...] = onehot(mm(spread(per), rank_b) == rank_of(per, base).astype(F32))
 
     blocks = CHUNK // LANES
-    rr, cc = iota((n_head, n_head), 0), iota((n_head, n_head), 1)
-    shuffle[...] = onehot(cc == (rr // tail % blocks) * n_tail + (rr // HEAD) * tail + rr % tail)
+    rr = iota((n_head, 1), 0)
+    shuffle[...] = onehot(
+        iota((n_head, n_head), 1) == (rr // tail % blocks) * n_tail + (rr // HEAD) * tail + rr % tail
+    )
 
     ld_og.wait()
 
@@ -239,17 +241,28 @@
 
         return carry
 
+    dispatch(0, 0)
+
+    grow = jnp.zeros((slots, LANES), F32)
+    for per, base, _, s_ref in parts:
+        n = slots * per
+        collect = onehot(iota((1, n), 1) // per == iota((slots, n), 0))
+        held = jnp.sum(s_ref[...].astype(F32) * mm(spread(per), gate_b), axis=1, keepdims=True)
+        put = jnp.where(iota((n, LANES), 1) == rank_of(per, base), held, 0.0)
+        grow = grow + mm(collect, put.astype(BF16))
+    for s in range(slots):
+        gate_out[s] = grow[s : s + 1, :]
     lax.fori_loop(1, slots, send_gate, 0)
     own_gate = pltpu.make_async_copy(gate_out.at[e], gate_in.at[e], ld_sem.at[3])
     own_gate.start()
-    lax.fori_loop(0, chunks, dispatch, 0)
+    lax.fori_loop(1, chunks, dispatch, 0)
 
     ld_h.wait()
     fb = min(256, hidden)
 
     def order(per, back):
         n = slots * per
-        r, c = iota((n, n), 0), iota((n, n), 1)
+        r, c = iota((n, 1), 0), iota((n, n), 1)
         if back:
             return onehot(c == (r % slots) * per + r // slots)
         return onehot(c == (r % per) * slots + r // per)
@@ -269,11 +282,9 @@
     await_bytes(gate_in.at[pl.ds(0, slots - 1)], gate_r)
     own_gate.wait()
     gin = gate_in[:, 0, :].astype(BF16)
-    for per, base, first in ((HEAD, 0, 0), (tail, HEAD, n_head)):
+    for per, base, first, _ in parts:
         n = slots * per
-        spread = onehot(iota((n, slots), 0) // per == iota((n, slots), 1))
-        c_of = iota((n, 1), 0) % per + base
-        picked = jnp.where(iota((n, LANES), 1) == c_of, mm(spread, gin), 0.0)
+        picked = jnp.where(iota((n, LANES), 1) == rank_of(per, base), mm(spread(per), gin), 0.0)
         gcol[first : first + n, :] = jnp.sum(picked, axis=1, keepdims=True)
     ld_w.wait()
     xb_rows = CORES * piece
@@ -291,13 +302,11 @@
 
     def from_y(c):
         await_bytes(yr.at[c], y_r.at[c])
+        came = [gsum[c, y].astype(F32)] + [yr[c, k - 1].astype(F32) for k in range(1, YS)]
         for h in range(2):
-            total = jnp.zeros((piece, ycols), F32)
-            for yy in range(YS):
-                came = gsum[c, y].astype(F32)
-                for k in range(1, YS):
-                    came = jnp.where(lax.rem(y + YS - k, YS) == yy, yr[c, k - 1].astype(F32), came)
-                total = total + y_weight[yy][h] * came
+            total = near_weight[0][h] * came[0]
+            for k in range(1, YS):
+                total = total + near_weight[k][h] * came[k]
             tb[c, :, h] = total.astype(BF16).reshape(zs, zrows, ycols)
         for k in range(1, zs):
             remote(tb.at[c, lax.rem(z + k, zs)], zr.at[c, k - 1], z_s.at[c], z_r.at[c], zdev(k))
@@ -327,6 +336,13 @@
         for yy in range(YS):
             cols = pl.ds(pl.multiple_of(c * CHUNK + yy * ycols, ycols), ycols)
             cg_ref[:, cols] = jnp.where(my_hot, ya[c, yy].astype(F32), gsum[c, yy].astype(F32)).astype(BF16)
+
+    def each(stage, start, stop):
+        def run(c, carry):
+            stage(c)
+            return carry
+
+        lax.fori_loop(start, stop, run, 0)
 
     def main(c, carry):
         await_bytes(rbuf.at[c, pl.ds(0, slots - 1)], row_r.at[c])
@@ -352,6 +368,10 @@
         lax.fori_loop(0, xs, partial, 0)
         remote(pb.at[c, 1 - core], pr.at[c], pair_s.at[c], pair_r.at[c], mate)
 
+        @pl.when(c == chunks - 1)
+        def _():
+            each(from_y, 0, chunks - 2)
+
         def accumulate(f, inner):
             rows = pl.ds(pl.multiple_of(f * fb, fb), fb)
             wcols = pl.ds(pl.multiple_of(c * CHUNK, CHUNK), CHUNK)
@@ -373,6 +393,9 @@
         return carry
 
     lax.fori_loop(0, chunks, main, 0)
+
+    from_x(chunks - 1)
+    each(from_y, chunks - 2, chunks)
 
     back_head, back_tail = order(HEAD, True), order(tail, True)
 
@@ -386,11 +409,10 @@
 
     score = lax.fori_loop(0, hidden // fb, finish, jnp.zeros((n_rows, 1), F32))
     srow = jnp.zeros((slots, LANES), F32)
-    for per, base, first in ((HEAD, 0, 0), (tail, HEAD, n_head)):
+    for per, base, first, _ in parts:
         n = slots * per
-        collect = jnp.where(iota((slots, n), 1) // per == iota((slots, n), 0), 1.0, 0.0)
-        c_of = iota((n, 1), 0) % per + base
-        put = jnp.where(iota((n, LANES), 1) == c_of, score[first : first + n, :], 0.0)
+        collect = jnp.where(iota((1, n), 1) // per == iota((slots, n), 0), 1.0, 0.0)
+        put = jnp.where(iota((n, LANES), 1) == rank_of(per, base), score[first : first + n, :], 0.0)
         srow = srow + lax.dot_general(
             collect, put, (((1,), (0,)), ((), ())), precision=lax.Precision.HIGHEST, preferred_element_type=F32
         )
@@ -407,19 +429,7 @@
     out_h = pltpu.make_async_copy(hg_v, hg_ref, ld_sem.at[5])
     out_h.start()
 
-    from_x(chunks - 1)
-
-    def each(stage):
-        def run(c, carry):
-            stage(c)
-            return carry
-
-        lax.fori_loop(0, chunks, run, 0)
-
-    each(from_y)
-    each(from_z)
-    each(from_v)
-    each(from_w)
+    each(from_z, 0, chunks)
 
     await_bytes(score_in.at[pl.ds(0, slots - 1)], score_r)
     own_score.wait()
@@ -429,6 +439,8 @@
         value = jnp.where(rank == float(c), sin[:, c : c + 1], value)
     for k in range(topk):
         rg_ref[k : k + 1, :] = jnp.sum(jnp.where(match(k), value, 0.0), axis=0, keepdims=True)
+    each(from_v, 0, chunks)
+    each(from_w, 0, chunks)
 
     out_h.wait()
     await_bytes(gate_out.at[pl.ds(0, slots - 1)], gate_s)

time: 164 us -> 157 us (0.957); the launches traced: 162 us -> 157 us
  Pallas kernels: 156 us -> 151 us
    pallas_call x1, Pallas kernels: 156 us -> 151 us  [local(): pl.pallas_call(functools.partial(kernel, dims), out_shape=(jax.ShapeDtype...]
where the time goes in v2:
time: 157 us
  Pallas kernels  151 us (96%)
  local copies, waits for them, and re-layouts  4.81 us (3%)
    pallas_call x1, Pallas kernels, local(): pl.pallas_call(functools.partial(kernel, dims), out_shape=(jax.ShapeDtype...  151 us
    unnamed x5, local copies, waits for them, and re-layouts  4.81 us

profile of v2, /device:TPU:2, one launch (start us, length us, event | category | flops | bytes accessed | tf_op | source)
XLA Modules:
  0.0 156.9 jit_solution(11502015230633619196)
XLA Ops:
  0.6 151.5 %expert_backward.1 = (f32[8,256]{1,0:T(8,128)}, bf16[640,1024]{1,0:T(8,128)(2,1)}, bf16[128,3584]{1,0:T(8,128)(2,1)}) custom-call(bf16[256,3584]{1,0:T(8,128)(2,1)} %og_hbm.1, bf16[1024,3584]{1,0:T(8,128)(2,1)} %bitcast.17, bf16[640,1024]{1,0:T(8,128)(2,1)} %bitcast.18, f32[8,256]{1,0:T(8,128)} %bitcast.21, s32[8,256]{1,0:T(8,128)} %bitcast.22, ...), custom_call_target="tpu_custom_call" | custom-call | tf_op jit(solution)/shard_map/expert_backward/pallas_call | solution.py:534
  152.1 1.3 copy.13
  153.4 0.0 copy-start
  153.4 2.6 %copy.14 = bf16[1,1,32,20,1024]{4,2,3,1,0:T(8,128)(2,1)} copy(bf16[1,1,32,20,1024]{4,2,3,1,0:T(8,128)(2,1)} %bitcast.19) | data formatting | bytes 2621440
  156.0 0.0 copy-done
  156.0 0.9 copy.15
Async XLA Ops:
  153.4 2.6 %copy-start = (bf16[128,3584]{1,0:T(8,128)(2,1)S(1)}, bf16[128,3584]{1,0:T(8,128)(2,1)}, u32[]{:S(2)}) copy-start(bf16[128,3584]{1,0:T(8,128)(2,1)} %get-tuple-element.8) | copy-start | bytes 2752516

commit v3 on v2

--- a/solution.py
+++ b/solution.py
@@ -394,9 +394,6 @@
 
     lax.fori_loop(0, chunks, main, 0)
 
-    from_x(chunks - 1)
-    each(from_y, chunks - 2, chunks)
-
     back_head, back_tail = order(HEAD, True), order(tail, True)
 
     def finish(f, score):
@@ -429,7 +426,11 @@
     out_h = pltpu.make_async_copy(hg_v, hg_ref, ld_sem.at[5])
     out_h.start()
 
-    each(from_z, 0, chunks)
+    each(from_y, chunks - 2, chunks - 1)
+    each(from_z, 0, chunks - 2)
+    from_x(chunks - 1)
+    each(from_y, chunks - 1, chunks)
+    each(from_z, chunks - 2, chunks)
 
     await_bytes(score_in.at[pl.ds(0, slots - 1)], score_r)
     own_score.wait()
@@ -457,6 +458,23 @@
         return carry
 
     lax.fori_loop(0, chunks, settle, 0)
+
+
+def emit(pieces, r_hbm, h_hbm, c_hbm, r_out, h_out, c_out, r_v, h_v, c_v, in_sem, out_sem):
+    rows = h_v.shape[0] // pieces
+    moves = [(r_hbm, r_v, r_out), (c_hbm, c_v, c_out)]
+    for i in range(pieces):
+        part = pl.ds(i * rows, rows)
+        moves.append((h_hbm.at[part], h_v.at[part], h_out.at[part]))
+    ins = [pltpu.make_async_copy(src, mid, in_sem.at[i]) for i, (src, mid, _) in enumerate(moves)]
+    outs = [pltpu.make_async_copy(mid, dst, out_sem.at[i]) for i, (_, mid, dst) in enumerate(moves)]
+    for one in ins:
+        one.start()
+    for first, then in zip(ins, outs):
+        first.wait()
+        then.start()
+    for one in outs:
+        one.wait()
 
 
 def local(groups, slots, out_grad, gates, routes, copy_pick, replica_plan, down_weight, saved_hidden):
@@ -546,6 +564,17 @@
         ),
         name="expert_backward",
     )(out_grad, down_weight[0], held, gates.T, routes.T, copy_pick.T, replica_plan[None, :])
+    shapes = (route_grad.shape, hidden_grad.shape, copy_grad.shape)
+    kinds = (F32, BF16, BF16)
+    pieces = 4
+    route_grad, hidden_grad, copy_grad = pl.pallas_call(
+        functools.partial(emit, pieces),
+        out_shape=tuple(jax.ShapeDtypeStruct(s, k) for s, k in zip(shapes, kinds)),
+        in_specs=[there, there, there],
+        out_specs=(there, there, there),
+        scratch_shapes=[vmem(s, k) for s, k in zip(shapes, kinds)] + [dma((pieces + 2,)), dma((pieces + 2,))],
+        name="results",
+    )(route_grad, hidden_grad, copy_grad)
     hidden_grad = hidden_grad.reshape(cap, slots, hidden).transpose(1, 0, 2)
     return route_grad.T, hidden_grad[None, None], copy_grad[None]
 

time: 157 us -> 153 us (0.975)
  local copies, waits for them, and re-layouts: 4.81 us -> 0 us
    unnamed x5 -> x0, local copies, waits for them, and re-layouts: 4.81 us -> none
    pallas_call x0 -> x1, Pallas kernels: none -> 2.65 us  [local(): pl.pallas_call(functools.partial(emit, pieces), out_shape=tuple((jax.Shap...]
    pallas_call x1, Pallas kernels: 151 us -> 149 us  [local(): pl.pallas_call(functools.partial(kernel, dims), out_shape=(jax.ShapeDtype...]
where the time goes in v3:
time: 153 us
  Pallas kernels  152 us (99%)
    pallas_call x1, Pallas kernels, local(): pl.pallas_call(functools.partial(kernel, dims), out_shape=(jax.ShapeDtype...  149 us

profile of v3, /device:TPU:2, one launch (start us, length us, event | category | flops | bytes accessed | tf_op | source)
XLA Modules:
  0.0 152.7 jit_solution(15208459911549733233)
XLA Ops:
  0.6 149.4 %expert_backward.1 = (f32[8,256]{1,0:T(8,128)}, bf16[640,1024]{1,0:T(8,128)(2,1)}, bf16[128,3584]{1,0:T(8,128)(2,1)}) custom-call(bf16[256,3584]{1,0:T(8,128)(2,1)} %og_hbm.1, bf16[1024,3584]{1,0:T(8,128)(2,1)} %bitcast.17, bf16[640,1024]{1,0:T(8,128)(2,1)} %bitcast.18, f32[8,256]{1,0:T(8,128)} %bitcast.19, s32[8,256]{1,0:T(8,128)} %bitcast.20, ...), custom_call_target="tpu_custom_call" | custom-call | tf_op jit(solution)/shard_map/expert_backward/pallas_call | solution.py:552
  150.1 2.6 %results.1 = (f32[8,256]{1,0:T(8,128)}, bf16[640,1024]{1,0:T(8,128)(2,1)}, bf16[128,3584]{1,0:T(8,128)(2,1)}) custom-call(f32[8,256]{1,0:T(8,128)} %get-tuple-element.9.r_hbm, bf16[640,1024]{1,0:T(8,128)(2,1)} %get-tuple-element.10.h_hbm, bf16[128,3584]{1,0:T(8,128)(2,1)} %get-tuple-element.11.c_hbm), custom_call_target="tpu_custom_call" | custom-call | tf_op jit(solution)/shard_map/results/pallas_call | solution.py:570

commit v4 on v3

--- a/solution.py
+++ b/solution.py
@@ -13,6 +13,9 @@
 HEAD = 16
 CHUNK = 512
 COLS = CHUNK + LANES
+PARTS = 1
+HALF = CHUNK // PARTS
+FIRST = 2
 MESH = pl.DeviceIdType.MESH
 F32 = jnp.float32
 BF16 = jnp.bfloat16
@@ -28,6 +31,11 @@
 
 def mm_nt(a, b):
     return lax.dot_general(a, b, (((1,), (1,)), ((), ())), preferred_element_type=F32)
+
+
+def groups_of(chunks):
+    cuts = [*range(0, chunks - 2, FIRST), chunks - 2, chunks - 1, chunks]
+    return list(zip(cuts, cuts[1:]))
 
 
 def onehot(mask):
@@ -62,6 +70,7 @@
     score_in,
     rows_b,
     scaled_b,
+    low_b,
     gcol,
     proj,
     hg_v,
@@ -289,65 +298,92 @@
     ld_w.wait()
     xb_rows = CORES * piece
 
-    def from_x(c):
-        await_bytes(xr.at[c], x_r.at[c])
-        total = xb[c, x].astype(F32)
+    def from_x(c, j):
+        await_bytes(xr.at[c, j], x_r.at[c, j])
+        total = xb[c, j, x].astype(F32)
         for k in range(xs - 1):
-            total = total + xr[c, k].astype(F32)
+            total = total + xr[c, j, k].astype(F32)
         total = total.astype(BF16)
-        for yy in range(YS):
-            gsum[c, yy] = total[:, yy * ycols : (yy + 1) * ycols]
-        for k in range(1, YS):
-            remote(gsum.at[c, lax.rem(y + k, YS)], yr.at[c, k - 1], y_s.at[c], y_r.at[c], ydev(k))
-
-    def from_y(c):
-        await_bytes(yr.at[c], y_r.at[c])
-        came = [gsum[c, y].astype(F32)] + [yr[c, k - 1].astype(F32) for k in range(1, YS)]
-        for h in range(2):
-            total = near_weight[0][h] * came[0]
-            for k in range(1, YS):
-                total = total + near_weight[k][h] * came[k]
-            tb[c, :, h] = total.astype(BF16).reshape(zs, zrows, ycols)
-        for k in range(1, zs):
-            remote(tb.at[c, lax.rem(z + k, zs)], zr.at[c, k - 1], z_s.at[c], z_r.at[c], zdev(k))
-
-    def from_z(c):
-        await_bytes(zr.at[c], z_r.at[c])
-        total = tb[c, z].astype(F32)
-        for k in range(zs - 1):
-            total = total + zr[c, k].astype(F32)
-        total = total.astype(BF16)
-        ub[c] = total
-        vb[c, z] = total
-        for k in range(1, zs):
-            remote(ub.at[c], vb.at[c, z], v_s.at[c], v_r.at[c], zdev(k))
-
-    def from_v(c):
-        await_bytes(vb.at[c, pl.ds(0, zs - 1)], v_r.at[c])
-        tables = [vb[c, :, h].reshape(piece, ycols).astype(F32) for h in range(2)]
-        for yy in range(YS):
-            wb[c, yy] = (y_weight[yy][0] * tables[0] + y_weight[yy][1] * tables[1]).astype(BF16)
-        ya[c, y] = wb[c, y]
-        for k in range(1, YS):
-            remote(wb.at[c, lax.rem(y + k, YS)], ya.at[c, y], w_s.at[c], w_r.at[c], ydev(k))
-
-    def from_w(c):
-        await_bytes(ya.at[c, pl.ds(0, YS - 1)], w_r.at[c])
-        for yy in range(YS):
-            cols = pl.ds(pl.multiple_of(c * CHUNK + yy * ycols, ycols), ycols)
-            cg_ref[:, cols] = jnp.where(my_hot, ya[c, yy].astype(F32), gsum[c, yy].astype(F32)).astype(BF16)
-
-    def each(stage, start, stop):
+        for i in range(YS // PARTS):
+            gsum[j * (YS // PARTS) + i, c] = total[:, i * ycols : (i + 1) * ycols]
+
+    stages = [(i,) + span for i, span in enumerate(groups_of(chunks))]
+    early = [stage for stage in stages if stage[2] <= chunks - 2]
+    middle = [stage for stage in stages if stage[2] == chunks - 1]
+    last = stages[-1]
+
+    def each(stage, lo, hi):
         def run(c, carry):
             stage(c)
             return carry
 
-        lax.fori_loop(start, stop, run, 0)
+        lax.fori_loop(lo, hi, run, 0)
+
+    def to_y(i, lo, hi):
+        span = pl.ds(lo, hi - lo)
+        for k in range(1, YS):
+            remote(gsum.at[lax.rem(y + k, YS), span], yr.at[k - 1, span], y_s.at[i], y_r.at[i], ydev(k))
+
+    def from_y(i, lo, hi):
+        span = pl.ds(lo, hi - lo)
+        await_bytes(yr.at[:, span], y_r.at[i])
+
+        def one(c):
+            came = [gsum[y, c].astype(F32)] + [yr[k - 1, c].astype(F32) for k in range(1, YS)]
+            for h in range(2):
+                total = near_weight[0][h] * came[0]
+                for k in range(1, YS):
+                    total = total + near_weight[k][h] * came[k]
+                tb[:, c, h] = total.astype(BF16).reshape(zs, zrows, ycols)
+
+        each(one, lo, hi)
+        for k in range(1, zs):
+            remote(tb.at[lax.rem(z + k, zs), span], zr.at[k - 1, span], z_s.at[i], z_r.at[i], zdev(k))
+
+    def from_z(i, lo, hi):
+        span = pl.ds(lo, hi - lo)
+        await_bytes(zr.at[:, span], z_r.at[i])
+
+        def one(c):
+            total = tb[z, c].astype(F32)
+            for k in range(zs - 1):
+                total = total + zr[k, c].astype(F32)
+            total = total.astype(BF16)
+            ub[c] = total
+            vb[z, c] = total
+
+        each(one, lo, hi)
+        for k in range(1, zs):
+            remote(ub.at[span], vb.at[z, span], v_s.at[i], v_r.at[i], zdev(k))
+
+    def from_v(i, lo, hi):
+        span = pl.ds(lo, hi - lo)
+        await_bytes(vb.at[pl.ds(0, zs - 1), span], v_r.at[i])
+
+        def one(c):
+            tables = [vb[:, c, h].reshape(piece, ycols).astype(F32) for h in range(2)]
+            for yy in range(YS):
+                wb[yy, c] = (y_weight[yy][0] * tables[0] + y_weight[yy][1] * tables[1]).astype(BF16)
+            ya[y, c] = wb[y, c]
+
+        each(one, lo, hi)
+        for k in range(1, YS):
+            remote(wb.at[lax.rem(y + k, YS), span], ya.at[y, span], w_s.at[i], w_r.at[i], ydev(k))
+
+    def from_w(i, lo, hi):
+        span = pl.ds(lo, hi - lo)
+        await_bytes(ya.at[pl.ds(0, YS - 1), span], w_r.at[i])
+
+        def one(c):
+            for yy in range(YS):
+                cols = pl.ds(pl.multiple_of(c * CHUNK + yy * ycols, ycols), ycols)
+                cg_ref[:, cols] = jnp.where(my_hot, ya[yy, c].astype(F32), gsum[yy, c].astype(F32)).astype(BF16)
+
+        each(one, lo, hi)
 
     def main(c, carry):
         await_bytes(rbuf.at[c, pl.ds(0, slots - 1)], row_r.at[c])
         pltpu.make_async_copy(sbuf.at[c, e], rbuf.at[c, e], own_sem.at[c]).wait()
-        rows_b[0:n_head, :] = rbuf[c, :, :, 0:CHUNK].reshape(n_head, CHUNK)
         low = lax.dot_general(
             shuffle[...],
             rbuf[c, :, :, CHUNK:COLS].reshape(n_head, LANES),
@@ -355,22 +391,27 @@
             preferred_element_type=F32,
         ).astype(BF16)
         for i in range(blocks):
-            rows_b[n_head:n_rows, i * LANES : (i + 1) * LANES] = low[i * n_tail : (i + 1) * n_tail, :]
-        scaled_b[...] = (gcol[...] * rows_b[...].astype(F32)).astype(BF16)
-
-        def partial(xx, inner):
-            rows = pl.ds(pl.multiple_of(xx * xb_rows, xb_rows), xb_rows)
-            out = mm(ht[rows, :], scaled_b[...]).astype(BF16)
-            for cc in range(CORES):
-                pb[c, cc, xx] = out[cc * piece : (cc + 1) * piece, :]
-            return inner
-
-        lax.fori_loop(0, xs, partial, 0)
-        remote(pb.at[c, 1 - core], pr.at[c], pair_s.at[c], pair_r.at[c], mate)
+            low_b[:, i * LANES : (i + 1) * LANES] = low[i * n_tail : (i + 1) * n_tail, :]
+        for j in range(PARTS):
+            cols = slice(j * HALF, (j + 1) * HALF)
+            rows_b[0:n_head, cols] = rbuf[c, :, :, cols].reshape(n_head, HALF)
+            rows_b[n_head:n_rows, cols] = low_b[:, cols]
+            scaled_b[...] = (gcol[...] * rows_b[:, cols].astype(F32)).astype(BF16)
+
+            def partial(xx, inner):
+                rows = pl.ds(pl.multiple_of(xx * xb_rows, xb_rows), xb_rows)
+                out = mm(ht[rows, :], scaled_b[...]).astype(BF16)
+                for cc in range(CORES):
+                    pb[c, j, cc, xx] = out[cc * piece : (cc + 1) * piece, :]
+                return inner
+
+            lax.fori_loop(0, xs, partial, 0)
+            remote(pb.at[c, j, 1 - core], pr.at[c, j], pair_s.at[c, j], pair_r.at[c, j], mate)
 
         @pl.when(c == chunks - 1)
         def _():
-            each(from_y, 0, chunks - 2)
+            for stage in early:
+                from_y(*stage)
 
         def accumulate(f, inner):
             rows = pl.ds(pl.multiple_of(f * fb, fb), fb)
@@ -380,15 +421,23 @@
 
         lax.fori_loop(0, hidden // fb, accumulate, 0)
 
-        await_bytes(pr.at[c], pair_r.at[c])
-        for xx in range(xs):
-            xb[c, xx] = (pb[c, core, xx].astype(F32) + pr[c, xx].astype(F32)).astype(BF16)
-        for k in range(1, xs):
-            remote(xb.at[c, lax.rem(x + k, xs)], xr.at[c, k - 1], x_s.at[c], x_r.at[c], xdev(k))
+        for j in range(PARTS):
+            await_bytes(pr.at[c, j], pair_r.at[c, j])
+            for xx in range(xs):
+                xb[c, j, xx] = (pb[c, j, core, xx].astype(F32) + pr[c, j, xx].astype(F32)).astype(BF16)
+            for k in range(1, xs):
+                remote(xb.at[c, j, lax.rem(x + k, xs)], xr.at[c, j, k - 1], x_s.at[c, j], x_r.at[c, j], xdev(k))
 
         @pl.when(c >= 1)
         def _():
-            from_x(c - 1)
+            for j in range(PARTS):
+                from_x(c - 1, j)
+
+        for stage in early + middle:
+
+            @pl.when(c == stage[2])
+            def _():
+                to_y(*stage)
 
         return carry
 
@@ -426,11 +475,21 @@
     out_h = pltpu.make_async_copy(hg_v, hg_ref, ld_sem.at[5])
     out_h.start()
 
-    each(from_y, chunks - 2, chunks - 1)
-    each(from_z, 0, chunks - 2)
-    from_x(chunks - 1)
-    each(from_y, chunks - 1, chunks)
-    each(from_z, chunks - 2, chunks)
+    for stage in middle:
+        from_y(*stage)
+    for stage in early:
+        from_z(*stage)
+    for j in range(PARTS):
+        from_x(chunks - 1, j)
+    to_y(*last)
+    for stage in early[:1]:
+        from_v(*stage)
+    from_y(*last)
+    for stage in middle:
+        from_z(*stage)
+    for stage in early[1:]:
+        from_v(*stage)
+    from_z(*last)
 
     await_bytes(score_in.at[pl.ds(0, slots - 1)], score_r)
     own_score.wait()
@@ -440,8 +499,12 @@
         value = jnp.where(rank == float(c), sin[:, c : c + 1], value)
     for k in range(topk):
         rg_ref[k : k + 1, :] = jnp.sum(jnp.where(match(k), value, 0.0), axis=0, keepdims=True)
-    each(from_v, 0, chunks)
-    each(from_w, 0, chunks)
+    for stage in middle:
+        from_v(*stage)
+    for stage in early + middle:
+        from_w(*stage)
+    from_v(*last)
+    from_w(*last)
 
     out_h.wait()
     await_bytes(gate_out.at[pl.ds(0, slots - 1)], gate_s)
@@ -449,15 +512,18 @@
 
     def settle(c, carry):
         await_bytes(sbuf.at[c, pl.ds(0, slots - 1)], row_s.at[c])
-        await_bytes(pr.at[c], pair_s.at[c])
-        await_bytes(xr.at[c], x_s.at[c])
-        await_bytes(yr.at[c], y_s.at[c])
-        await_bytes(zr.at[c], z_s.at[c])
-        await_bytes(zr.at[c], v_s.at[c])
-        await_bytes(yr.at[c], w_s.at[c])
+        for j in range(PARTS):
+            await_bytes(pr.at[c, j], pair_s.at[c, j])
+            await_bytes(xr.at[c, j], x_s.at[c, j])
         return carry
 
     lax.fori_loop(0, chunks, settle, 0)
+    for i, lo, hi in stages:
+        span = pl.ds(lo, hi - lo)
+        await_bytes(yr.at[:, span], y_s.at[i])
+        await_bytes(zr.at[:, span], z_s.at[i])
+        await_bytes(zr.at[:, span], v_s.at[i])
+        await_bytes(yr.at[:, span], w_s.at[i])
 
 
 def emit(pieces, r_hbm, h_hbm, c_hbm, r_out, h_out, c_out, r_v, h_v, c_v, in_sem, out_sem):
@@ -509,40 +575,41 @@
         vmem((slots, 1, LANES), F32),
         vmem((slots, 1, LANES), F32),
         vmem((n_rows, CHUNK), BF16),
-        vmem((n_rows, CHUNK), BF16),
+        vmem((n_rows, HALF), BF16),
+        vmem((slots * tail, CHUNK), BF16),
         vmem((n_rows, 1), F32),
         vmem((n_rows, hidden), F32),
         vmem((n_rows, hidden), BF16),
-        vmem((chunks, CORES, xs, piece, CHUNK), BF16),
-        vmem((chunks, xs, piece, CHUNK), BF16),
-        vmem((chunks, xs, piece, CHUNK), BF16),
-        vmem((chunks, xs - 1, piece, CHUNK), BF16),
-        vmem((chunks, YS, piece, ycols), BF16),
-        vmem((chunks, YS - 1, piece, ycols), BF16),
-        vmem((chunks, zs, 2, zrows, ycols), BF16),
-        vmem((chunks, zs - 1, 2, zrows, ycols), BF16),
+        vmem((chunks, PARTS, CORES, xs, piece, HALF), BF16),
+        vmem((chunks, PARTS, xs, piece, HALF), BF16),
+        vmem((chunks, PARTS, xs, piece, HALF), BF16),
+        vmem((chunks, PARTS, xs - 1, piece, HALF), BF16),
+        vmem((YS, chunks, piece, ycols), BF16),
+        vmem((YS - 1, chunks, piece, ycols), BF16),
+        vmem((zs, chunks, 2, zrows, ycols), BF16),
+        vmem((zs - 1, chunks, 2, zrows, ycols), BF16),
         vmem((chunks, 2, zrows, ycols), BF16),
-        vmem((chunks, zs, 2, zrows, ycols), BF16),
-        vmem((chunks, YS, piece, ycols), BF16),
-        vmem((chunks, YS, piece, ycols), BF16),
+        vmem((zs, chunks, 2, zrows, ycols), BF16),
+        vmem((YS, chunks, piece, ycols), BF16),
+        vmem((YS, chunks, piece, ycols), BF16),
         dma((6,)),
         dma((chunks,)),
         dma((chunks,)),
         dma((chunks,)),
         dma,
         dma,
-        dma((chunks,)),
-        dma((chunks,)),
-        dma((chunks,)),
-        dma((chunks,)),
-        dma((chunks,)),
-        dma((chunks,)),
-        dma((chunks,)),
-        dma((chunks,)),
-        dma((chunks,)),
-        dma((chunks,)),
-        dma((chunks,)),
-        dma((chunks,)),
+        dma((chunks, PARTS)),
+        dma((chunks, PARTS)),
+        dma((chunks, PARTS)),
+        dma((chunks, PARTS)),
+        dma((len(groups_of(chunks)),)),
+        dma((len(groups_of(chunks)),)),
+        dma((len(groups_of(chunks)),)),
+        dma((len(groups_of(chunks)),)),
+        dma((len(groups_of(chunks)),)),
+        dma((len(groups_of(chunks)),)),
+        dma((len(groups_of(chunks)),)),
+        dma((len(groups_of(chunks)),)),
         dma,
         dma,
     ]

time: 153 us -> 151 us (0.987)
  Pallas kernels: 152 us -> 149 us
    pallas_call x1, Pallas kernels: 149 us -> 147 us  [local(): pl.pallas_call(functools.partial(kernel, dims), out_shape=(jax.ShapeDtype...]
where the time goes in v4:
time: 151 us; the launch traced here: 150 us
  Pallas kernels  149 us (99%)
    pallas_call x1, Pallas kernels, local(): pl.pallas_call(functools.partial(kernel, dims), out_shape=(jax.ShapeDtype...  147 us

profile of v4, /device:TPU:2, one launch (start us, length us, event | category | flops | bytes accessed | tf_op | source)
XLA Modules:
  0.0 150.0 jit_solution(15715485771053857475)
XLA Ops:
  0.6 146.8 %expert_backward.1 = (f32[8,256]{1,0:T(8,128)}, bf16[640,1024]{1,0:T(8,128)(2,1)}, bf16[128,3584]{1,0:T(8,128)(2,1)}) custom-call(bf16[256,3584]{1,0:T(8,128)(2,1)} %og_hbm.1, bf16[1024,3584]{1,0:T(8,128)(2,1)} %bitcast.17, bf16[640,1024]{1,0:T(8,128)(2,1)} %bitcast.18, f32[8,256]{1,0:T(8,128)} %bitcast.19, s32[8,256]{1,0:T(8,128)} %bitcast.20, ...), custom_call_target="tpu_custom_call" | custom-call | tf_op jit(solution)/shard_map/expert_backward/pallas_call | solution.py:619
  147.4 2.6 %results.1 = (f32[8,256]{1,0:T(8,128)}, bf16[640,1024]{1,0:T(8,128)(2,1)}, bf16[128,3584]{1,0:T(8,128)(2,1)}) custom-call(f32[8,256]{1,0:T(8,128)} %get-tuple-element.9.r_hbm, bf16[640,1024]{1,0:T(8,128)(2,1)} %get-tuple-element.10.h_hbm, bf16[128,3584]{1,0:T(8,128)(2,1)} %get-tuple-element.11.c_hbm), custom_call_target="tpu_custom_call" | custom-call | tf_op jit(solution)/shard_map/results/pallas_call | solution.py:637

commit v5 on v4

--- a/solution.py
+++ b/solution.py
@@ -73,7 +73,6 @@
     low_b,
     gcol,
     proj,
-    hg_v,
     pb,
     pr,
     xb,
@@ -449,8 +448,8 @@
         cols = pl.ds(pl.multiple_of(f * fb, fb), fb)
         block = proj[:, cols]
         grad = (gcol[...] * block).astype(BF16)
-        hg_v[0:n_head, cols] = mm(back_head, grad[0:n_head, :]).astype(BF16)
-        hg_v[n_head:n_rows, cols] = mm(back_tail, grad[n_head:n_rows, :]).astype(BF16)
+        hg_ref[0:n_head, cols] = mm(back_head, grad[0:n_head, :]).astype(BF16)
+        hg_ref[n_head:n_rows, cols] = mm(back_tail, grad[n_head:n_rows, :]).astype(BF16)
         return score + jnp.sum(block * hq[:, cols].astype(F32), axis=1, keepdims=True)
 
     score = lax.fori_loop(0, hidden // fb, finish, jnp.zeros((n_rows, 1), F32))
@@ -472,8 +471,6 @@
     lax.fori_loop(1, slots, send_score, 0)
     own_score = pltpu.make_async_copy(score_out.at[e], score_in.at[e], ld_sem.at[4])
     own_score.start()
-    out_h = pltpu.make_async_copy(hg_v, hg_ref, ld_sem.at[5])
-    out_h.start()
 
     for stage in middle:
         from_y(*stage)
@@ -506,7 +503,6 @@
     from_v(*last)
     from_w(*last)
 
-    out_h.wait()
     await_bytes(gate_out.at[pl.ds(0, slots - 1)], gate_s)
     await_bytes(score_out.at[pl.ds(0, slots - 1)], score_s)
 
@@ -526,20 +522,14 @@
         await_bytes(yr.at[:, span], w_s.at[i])
 
 
-def emit(pieces, r_hbm, h_hbm, c_hbm, r_out, h_out, c_out, r_v, h_v, c_v, in_sem, out_sem):
-    rows = h_v.shape[0] // pieces
-    moves = [(r_hbm, r_v, r_out), (c_hbm, c_v, c_out)]
-    for i in range(pieces):
-        part = pl.ds(i * rows, rows)
-        moves.append((h_hbm.at[part], h_v.at[part], h_out.at[part]))
-    ins = [pltpu.make_async_copy(src, mid, in_sem.at[i]) for i, (src, mid, _) in enumerate(moves)]
-    outs = [pltpu.make_async_copy(mid, dst, out_sem.at[i]) for i, (_, mid, dst) in enumerate(moves)]
-    for one in ins:
+def emit(r_v, h_v, c_v, r_out, h_out, c_out, sem):
+    moves = [
+        pltpu.make_async_copy(src, dst, sem.at[i])
+        for i, (src, dst) in enumerate(((h_v, h_out), (c_v, c_out), (r_v, r_out)))
+    ]
+    for one in moves:
         one.start()
-    for first, then in zip(ins, outs):
-        first.wait()
-        then.start()
-    for one in outs:
+    for one in moves:
         one.wait()
 
 
@@ -579,7 +569,6 @@
         vmem((slots * tail, CHUNK), BF16),
         vmem((n_rows, 1), F32),
         vmem((n_rows, hidden), F32),
-        vmem((n_rows, hidden), BF16),
         vmem((chunks, PARTS, CORES, xs, piece, HALF), BF16),
         vmem((chunks, PARTS, xs, piece, HALF), BF16),
         vmem((chunks, PARTS, xs, piece, HALF), BF16),
@@ -618,30 +607,25 @@
     there = pl.BlockSpec(memory_space=pl.ANY)
     route_grad, hidden_grad, copy_grad = pl.pallas_call(
         functools.partial(kernel, dims),
-        out_shape=(
-            jax.ShapeDtypeStruct((topk, toks), F32),
-            jax.ShapeDtypeStruct((n_rows, hidden), BF16),
-            jax.ShapeDtypeStruct((piece, width), BF16),
-        ),
+        out_shape=(vmem((topk, toks), F32), vmem((n_rows, hidden), BF16), vmem((piece, width), BF16)),
         in_specs=[there, there, there, here, here, here, here],
-        out_specs=(here, there, here),
+        out_specs=(here, here, here),
         scratch_shapes=scratch,
         compiler_params=pltpu.CompilerParams(
-            collective_id=0, has_side_effects=True, vmem_limit_bytes=63 * 2**20
+            collective_id=0, has_side_effects=True, vmem_limit_bytes=58 * 2**20
         ),
         name="expert_backward",
     )(out_grad, down_weight[0], held, gates.T, routes.T, copy_pick.T, replica_plan[None, :])
     shapes = (route_grad.shape, hidden_grad.shape, copy_grad.shape)
     kinds = (F32, BF16, BF16)
-    pieces = 4
     route_grad, hidden_grad, copy_grad = pl.pallas_call(
-        functools.partial(emit, pieces),
+        emit,
         out_shape=tuple(jax.ShapeDtypeStruct(s, k) for s, k in zip(shapes, kinds)),
-        in_specs=[there, there, there],
+        in_specs=[here, here, here],
         out_specs=(there, there, there),
-        scratch_shapes=[vmem(s, k) for s, k in zip(shapes, kinds)] + [dma((pieces + 2,)), dma((pieces + 2,))],
+        scratch_shapes=[dma((3,))],
         name="results",
-    )(route_grad, hidden_grad, copy_grad)
+    )(*[pltpu.with_memory_space_constraint(a, pltpu.VMEM) for a in (route_grad, hidden_grad, copy_grad)])
     hidden_grad = hidden_grad.reshape(cap, slots, hidden).transpose(1, 0, 2)
     return route_grad.T, hidden_grad[None, None], copy_grad[None]
 

time: 151 us -> 148 us (0.980)
  Pallas kernels: 149 us -> 147 us
    pallas_call x2, Pallas kernels: 149 us -> 147 us  [the longest x1 146 us: local(): pl.pallas_call(functools.partial(kernel, dims), out_shape=(vmem((topk, to...]
where the time goes in v5:
time: 148 us
  Pallas kernels  147 us (99%)
    pallas_call x1, Pallas kernels, local(): pl.pallas_call(functools.partial(kernel, dims), out_shape=(vmem((topk, to...  146 us

profile of v5, /device:TPU:2, one launch (start us, length us, event | category | flops | bytes accessed | tf_op | source)
XLA Modules:
  0.0 147.8 jit_solution(4978114758586885372)
XLA Ops:
  0.6 145.8 %expert_backward.1 = (f32[8,256]{1,0:T(8,128)S(1)}, bf16[640,1024]{1,0:T(8,128)(2,1)S(1)}, bf16[128,3584]{1,0:T(8,128)(2,1)S(1)}) custom-call(bf16[256,3584]{1,0:T(8,128)(2,1)} %og_hbm.1, bf16[1024,3584]{1,0:T(8,128)(2,1)} %bitcast.17, bf16[640,1024]{1,0:T(8,128)(2,1)} %bitcast.18, f32[8,256]{1,0:T(8,128)} %bitcast.19, s32[8,256]{1,0:T(8,128)} %bitcast.20, ...), custom_call_target="tpu_custom_call" | custom-call | tf_op jit(solution)/shard_map/expert_backward/pallas_call | solution.py:608
  146.4 1.4 results.1

commit v6 on v5

--- a/solution.py
+++ b/solution.py
@@ -468,17 +468,16 @@
         remote(score_out.at[plane_slot(k)], score_in.at[e], score_s, score_r, plane(k))
         return carry
 
+    for stage in middle:
+        from_y(*stage)
+    for j in range(PARTS):
+        from_x(chunks - 1, j)
+    to_y(*last)
+    for stage in early:
+        from_z(*stage)
     lax.fori_loop(1, slots, send_score, 0)
     own_score = pltpu.make_async_copy(score_out.at[e], score_in.at[e], ld_sem.at[4])
     own_score.start()
-
-    for stage in middle:
-        from_y(*stage)
-    for stage in early:
-        from_z(*stage)
-    for j in range(PARTS):
-        from_x(chunks - 1, j)
-    to_y(*last)
     for stage in early[:1]:
         from_v(*stage)
     from_y(*last)

time: 148 us -> 151 us (1.020)
  Pallas kernels: 147 us -> 149 us
    pallas_call x1, Pallas kernels: 146 us -> 148 us  [local(): pl.pallas_call(functools.partial(kernel, dims), out_shape=(vmem((topk, to...]
where the time goes in v6:
time: 151 us; the launch traced here: 150 us
  Pallas kernels  149 us (99%)
    pallas_call x1, Pallas kernels, local(): pl.pallas_call(functools.partial(kernel, dims), out_shape=(vmem((topk, to...  148 us

profile of v6, /device:TPU:2, one launch (start us, length us, event | category | flops | bytes accessed | tf_op | source)
XLA Modules:
  0.0 150.0 jit_solution(5370888320693516977)
XLA Ops:
  0.6 148.0 %expert_backward.1 = (f32[8,256]{1,0:T(8,128)S(1)}, bf16[640,1024]{1,0:T(8,128)(2,1)S(1)}, bf16[128,3584]{1,0:T(8,128)(2,1)S(1)}) custom-call(bf16[256,3584]{1,0:T(8,128)(2,1)} %og_hbm.1, bf16[1024,3584]{1,0:T(8,128)(2,1)} %bitcast.17, bf16[640,1024]{1,0:T(8,128)(2,1)} %bitcast.18, f32[8,256]{1,0:T(8,128)} %bitcast.19, s32[8,256]{1,0:T(8,128)} %bitcast.20, ...), custom_call_target="tpu_custom_call" | custom-call | tf_op jit(solution)/shard_map/expert_backward/pallas_call | solution.py:607
  148.7 1.4 results.1
